TPU v7x, 32 devices: a whole 2x2x4 slice. The times are simulated.
32 devices in a mesh: dp: 4 (over x, core), seq: 2 (over y), fsdp: 4 (over z).
Axes of the slice: x: 2, y: 2, z: 4, core: 2. Of those that a mesh axis runs over, the one named last changes fastest.
Arguments:
- tokens: bfloat16 [16, 1536, 768], P(('dp', 'fsdp'), 'seq'), may hold values from -6 to 6
- attn_in: bfloat16 [768, 2304], P('fsdp'), may hold values from -0.21875 to 0.21875
- attn_out: bfloat16 [768, 768], P('fsdp'), may hold values from -1.75 to 1.75
- router: bfloat16 [768, 4], P('fsdp'), may hold values from -0.15625 to 0.15625
- gains: bfloat16 [768, 2], P('fsdp'), may hold values from 0.5 to 1.5
- expert_w: bfloat16 [3072, 4, 1536], P('fsdp'), may hold values from -0.21875 to 0.21875
- expert_ids: int32 [16, 1536, 2], P(('dp', 'fsdp'), 'seq'), may hold values from 0 to 3, all different within a row
- segments: int32 [16, 512], P(('dp', 'fsdp')), may hold values from 0 to 1, as said below
- cotangent: bfloat16 [16, 1536, 768], P(('dp', 'fsdp'), 'seq'), may hold values from -6 to 6
Outputs:
- block_out: bfloat16 [16, 1536, 768], P(('dp', 'fsdp'), 'seq')
- d_tokens: bfloat16 [16, 1536, 768], P(('dp', 'fsdp'), 'seq')
- d_attn_in: float32 [768, 2304], P('fsdp')
- d_attn_out: float32 [768, 768], P('fsdp')
- d_router: float32 [768, 4], P('fsdp')
- d_gains: float32 [768, 2], P('fsdp')
- d_expert: float32 [3072, 4, 1536], P('fsdp')
Inputs may be any that keep to these rules, and one draw needn't show every extreme that they name: `expert_ids`: the two experts of a token differ. `segments`: never falls along a group; every continuation has 64 to 384 tokens, and in every group one has exactly 384.
All inputs are finite; a program needn't handle non-finite values.
Results may differ from a plain program's by a relative error of at most 0.018.
Values may be sent and summed in bfloat16 or wider, within the bound.
A program may use at most 384 MiB of HBM per device.

v0:
```python
import jax
import jax.numpy as jnp
from jax import lax
from jax.sharding import PartitionSpec as P

HEADS = 12
HEAD_DIM = 64
EXPERTS = 4
PROMPT = 1024


EPSILON = 1e-06
NEGATIVE = -1e30
HIGH = lax.Precision.HIGHEST


def route(choose, capacity, experts_count):
    pair_expert = choose.reshape(-1)
    one_hot = (pair_expert[:, None] == jnp.arange(experts_count, dtype=jnp.int32)[None, :]).astype(
        jnp.int32
    )
    before = jnp.cumsum(one_hot, axis=0) - one_hot
    place = jnp.sum(before * one_hot, axis=1)
    kept = place < capacity
    slots = jnp.where(kept, pair_expert * capacity + place, experts_count * capacity)
    pair_count = pair_expert.shape[0]
    pair_of = (
        jnp.zeros((experts_count * capacity + 1,), jnp.int32)
        .at[slots]
        .set(jnp.arange(pair_count, dtype=jnp.int32))
    )
    filled = (
        jnp.zeros((experts_count * capacity + 1,), jnp.int32)
        .at[slots]
        .set(jnp.ones((pair_count,), jnp.int32))
    )
    return (slots, kept, pair_of[:-1], filled[:-1] > 0)


def expert_pre(expert_in, piece):
    width = piece.shape[2] // 2
    return jnp.einsum(
        "ecd,fed->ecf", expert_in, piece[:, :, :width], preferred_element_type=jnp.float32
    )


def expert_out(activity, piece):
    width = piece.shape[2] // 2
    return jnp.einsum(
        "ecf,fed->ecd", activity, piece[:, :, width:], preferred_element_type=jnp.float32
    )


def expert_back(grad_result, pre_rows, piece):
    width = piece.shape[2] // 2
    grad_act = jnp.einsum(
        "ecd,fed->ecf", grad_result, piece[:, :, width:], preferred_element_type=jnp.float32
    )
    grad_pre = jax.vjp(jax.nn.gelu, pre_rows)[1](grad_act)[0].astype(jnp.bfloat16)
    grad_in = jnp.einsum(
        "ecf,fed->ecd", grad_pre, piece[:, :, :width], preferred_element_type=jnp.float32
    )
    return (grad_pre, grad_in)


def shards(tokens, attn_in, attn_out, router, gains, expert_w, expert_ids, segments, cotangent):
    x_rows = tokens[0].astype(jnp.float32)
    tok_rows = x_rows.shape[0]
    width = x_rows.shape[1]
    seq_count = lax.axis_size("seq")
    scale = HEAD_DIM ** (-0.5)
    w_qkv, w_proj, w_route, gain_pair = (
        lax.all_gather(attn_in, "fsdp", axis=0, tiled=True),
        lax.all_gather(attn_out, "fsdp", axis=0, tiled=True),
        lax.all_gather(router, "fsdp", axis=0, tiled=True),
        lax.all_gather(gains, "fsdp", axis=0, tiled=True),
    )
    gain_f = gain_pair.astype(jnp.float32)
    r_one = lax.rsqrt(jnp.mean(x_rows * x_rows, axis=-1, keepdims=True) + EPSILON)
    normed_one = x_rows * r_one
    normed_low = (normed_one * gain_f[:, 0]).astype(jnp.bfloat16)
    projected = jnp.dot(normed_low, w_qkv, preferred_element_type=jnp.float32).astype(jnp.bfloat16)
    local_heads = HEADS // seq_count
    head_cols = local_heads * HEAD_DIM
    arrived = lax.all_to_all(
        projected.reshape(tok_rows, 3, seq_count, head_cols),
        "seq",
        split_axis=2,
        concat_axis=0,
        tiled=True,
    )
    group_len = arrived.shape[0]
    queries = arrived[:, 0, 0].reshape(group_len, local_heads, HEAD_DIM)
    keys = arrived[:, 1, 0].reshape(group_len, local_heads, HEAD_DIM)
    values = arrived[:, 2, 0].reshape(group_len, local_heads, HEAD_DIM)
    seg_full = jnp.concatenate([jnp.full((PROMPT,), -1, jnp.int32), segments[0]])
    block = min(512, group_len)
    key_place = jnp.arange(group_len, dtype=jnp.int32)
    begins = jnp.arange(group_len // block, dtype=jnp.int32) * block

    def block_scores(begin):
        query_block = lax.dynamic_slice_in_dim(queries, begin, block, 0)
        query_place = begin + jnp.arange(block, dtype=jnp.int32)
        query_seg = lax.dynamic_slice_in_dim(seg_full, begin, block, 0)
        raw = (
            jnp.einsum("qhd,khd->hqk", query_block, keys, preferred_element_type=jnp.float32)
            * scale
        )
        allowed = (key_place[None, :] <= query_place[:, None]) & (
            (seg_full[None, :] < 0) | (seg_full[None, :] == query_seg[:, None])
        )
        return (jnp.where(allowed[None], raw, NEGATIVE), query_block)

    def forward_block(begin):
        masked, query_block = block_scores(begin)
        row_max = jnp.max(masked, axis=-1, keepdims=True)
        expo = jnp.exp(masked - row_max)
        row_total = jnp.sum(expo, axis=-1, keepdims=True)
        probs = expo / row_total
        mixed_block = jnp.einsum(
            "hqk,khd->qhd", probs.astype(jnp.bfloat16), values, preferred_element_type=jnp.float32
        )
        return (mixed_block.astype(jnp.bfloat16), (row_max + jnp.log(row_total))[:, :, 0])

    mixed_blocks, log_totals = lax.map(forward_block, begins)
    mixed_heads = mixed_blocks.reshape(group_len, 1, head_cols)
    returned = lax.all_to_all(mixed_heads, "seq", split_axis=0, concat_axis=1, tiled=True)
    attended = returned.reshape(tok_rows, width)
    hidden = x_rows + jnp.dot(attended, w_proj, preferred_element_type=jnp.float32)
    r_two = lax.rsqrt(jnp.mean(hidden * hidden, axis=-1, keepdims=True) + EPSILON)
    normed_two = hidden * r_two
    routed_low = (normed_two * gain_f[:, 1]).astype(jnp.bfloat16)
    logits = jnp.dot(routed_low, w_route, preferred_element_type=jnp.float32)
    probs_r = jax.nn.softmax(logits, axis=-1)
    choose = expert_ids[0]
    choose_map = (choose[:, :, None] == jnp.arange(EXPERTS, dtype=jnp.int32)[None, None, :]).astype(
        jnp.float32
    )
    gates = jnp.sum(probs_r[:, None, :] * choose_map, axis=-1)
    capacity = 2 * tok_rows // EXPERTS
    slots, kept, pair_of, filled = route(choose, capacity, EXPERTS)
    token_of = pair_of // 2
    expert_in = jnp.where(
        filled[:, None], routed_low[token_of], jnp.zeros((), jnp.bfloat16)
    ).reshape(EXPERTS, capacity, width)
    piece = lax.all_gather(expert_w, "fsdp", axis=0, tiled=True)
    pre_rows = expert_pre(expert_in, piece)
    result = expert_out(jax.nn.gelu(pre_rows).astype(jnp.bfloat16), piece)
    padded = jnp.concatenate(
        [result.reshape(EXPERTS * capacity, width), jnp.zeros((1, width), jnp.float32)], axis=0
    )
    picked = padded[slots].reshape(tok_rows, 2, width)
    kept_f = kept.astype(jnp.float32).reshape(tok_rows, 2)
    weight_pair = gates * kept_f
    block_out = hidden + jnp.sum(weight_pair[..., None] * picked, axis=1)
    grad_out_rows = cotangent[0].astype(jnp.float32)
    grad_gates = kept_f * jnp.sum(grad_out_rows[:, None, :] * picked, axis=-1)
    grad_probs = jnp.sum(grad_gates[:, :, None] * choose_map, axis=1)
    grad_logits = probs_r * (grad_probs - jnp.sum(probs_r * grad_probs, axis=-1, keepdims=True))
    grad_route_w = jnp.dot(routed_low.astype(jnp.float32).T, grad_logits, precision=HIGH)
    grad_routed = jnp.dot(grad_logits, w_route.astype(jnp.float32).T, precision=HIGH)
    scaled = (weight_pair[:, :, None] * grad_out_rows[:, None, :]).reshape(2 * tok_rows, width)
    grad_result = (
        jnp.where(filled[:, None], scaled[pair_of], 0.0)
        .astype(jnp.bfloat16)
        .reshape(EXPERTS, capacity, width)
    )
    piece = lax.all_gather(expert_w, "fsdp", axis=0, tiled=True)
    pre_rows = expert_pre(expert_in, piece)
    act_rows = jax.nn.gelu(pre_rows).astype(jnp.bfloat16)
    grad_pre_rows, grad_in_rows = expert_back(grad_result, pre_rows, piece)
    act_store = act_rows
    pre_rows = grad_pre_rows
    act_rows = act_store
    grad_first = jnp.einsum("ecd,ecf->fed", expert_in, pre_rows, preferred_element_type=jnp.float32)
    grad_second = jnp.einsum(
        "ecf,ecd->fed", act_rows, grad_result, preferred_element_type=jnp.float32
    )
    expert_shard = lax.psum_scatter(
        jnp.concatenate([grad_first, grad_second], axis=2).astype(jnp.bfloat16),
        "fsdp",
        scatter_dimension=0,
        tiled=True,
    )
    padded_in = jnp.concatenate(
        [grad_in_rows.reshape(EXPERTS * capacity, width), jnp.zeros((1, width), jnp.float32)],
        axis=0,
    )
    grad_routed = grad_routed + jnp.sum(padded_in[slots].reshape(tok_rows, 2, width), axis=1)
    grad_gain_two = jnp.sum(grad_routed * normed_two, axis=0)
    scaled_two = grad_routed * gain_f[:, 1]
    grad_hidden = grad_out_rows + r_two * (
        scaled_two - normed_two * jnp.mean(scaled_two * normed_two, axis=-1, keepdims=True)
    )
    hid_low = grad_hidden.astype(jnp.bfloat16)
    grad_proj_w = jnp.dot(attended.T, hid_low, preferred_element_type=jnp.float32)
    grad_attended = jnp.dot(hid_low, w_proj.T, preferred_element_type=jnp.float32).astype(
        jnp.bfloat16
    )
    grad_heads = lax.all_to_all(
        grad_attended.reshape(tok_rows, seq_count, head_cols),
        "seq",
        split_axis=1,
        concat_axis=0,
        tiled=True,
    )
    grad_mixed = grad_heads.reshape(group_len, local_heads, HEAD_DIM)

    def back_block(carry, inputs):
        begin, log_rows = inputs
        masked, query_block = block_scores(begin)
        probs = jnp.exp(masked - log_rows[:, :, None])
        grad_block = lax.dynamic_slice_in_dim(grad_mixed, begin, block, 0)
        grad_p = jnp.einsum("qhd,khd->hqk", grad_block, values, preferred_element_type=jnp.float32)
        inner = jnp.sum(probs * grad_p, axis=-1, keepdims=True)
        grad_scores = (probs * (grad_p - inner)).astype(jnp.bfloat16)
        grad_query = (
            jnp.einsum("hqk,khd->qhd", grad_scores, keys, preferred_element_type=jnp.float32)
            * scale
        )
        grad_key = (
            carry[0]
            + jnp.einsum(
                "hqk,qhd->khd", grad_scores, query_block, preferred_element_type=jnp.float32
            )
            * scale
        )
        grad_value = carry[1] + jnp.einsum(
            "hqk,qhd->khd",
            probs.astype(jnp.bfloat16),
            grad_block,
            preferred_element_type=jnp.float32,
        )
        return ((grad_key, grad_value), grad_query)

    zero_heads = jnp.zeros((group_len, local_heads, HEAD_DIM), jnp.float32)
    (grad_keys, grad_values), grad_queries = lax.scan(
        back_block, (zero_heads, zero_heads), (begins, log_totals)
    )
    stacked = jnp.stack(
        [
            grad_queries.reshape(group_len, head_cols),
            grad_keys.reshape(group_len, head_cols),
            grad_values.reshape(group_len, head_cols),
        ],
        axis=1,
    )
    stacked = stacked.astype(jnp.bfloat16).reshape(group_len, 3, 1, head_cols)
    grad_back = lax.all_to_all(stacked, "seq", split_axis=0, concat_axis=2, tiled=True)
    grad_proj_rows = grad_back.reshape(tok_rows, 3 * width)
    grad_qkv_w = jnp.dot(normed_low.T, grad_proj_rows, preferred_element_type=jnp.float32)
    grad_normed = jnp.dot(grad_proj_rows, w_qkv.T, preferred_element_type=jnp.float32)
    grad_gain_one = jnp.sum(grad_normed * normed_one, axis=0)
    scaled_one = grad_normed * gain_f[:, 0]
    grad_x = grad_hidden + r_one * (
        scaled_one - normed_one * jnp.mean(scaled_one * normed_one, axis=-1, keepdims=True)
    )
    grad_gains = jnp.stack([grad_gain_one, grad_gain_two], axis=1)
    shard_qkv, shard_proj, shard_route, shard_gains = (
        lax.psum_scatter(
            grad_qkv_w.astype(jnp.bfloat16), "fsdp", scatter_dimension=0, tiled=True
        ).astype(jnp.float32),
        lax.psum_scatter(
            grad_proj_w.astype(jnp.bfloat16), "fsdp", scatter_dimension=0, tiled=True
        ).astype(jnp.float32),
        lax.psum_scatter(
            grad_route_w.astype(jnp.bfloat16), "fsdp", scatter_dimension=0, tiled=True
        ).astype(jnp.float32),
        lax.psum_scatter(
            grad_gains.astype(jnp.bfloat16), "fsdp", scatter_dimension=0, tiled=True
        ).astype(jnp.float32),
    )
    part_qkv, part_proj, part_expert = (
        lax.psum_scatter(
            shard_qkv.astype(jnp.bfloat16), ("dp", "seq"), scatter_dimension=1, tiled=True
        ).astype(jnp.float32),
        lax.psum_scatter(
            shard_proj.astype(jnp.bfloat16), ("dp", "seq"), scatter_dimension=1, tiled=True
        ).astype(jnp.float32),
        lax.psum_scatter(expert_shard, ("dp", "seq"), scatter_dimension=2, tiled=True).astype(
            jnp.float32
        ),
    )
    summed_qkv, summed_proj, summed_expert = (
        lax.all_gather(part_qkv.astype(jnp.bfloat16), ("dp", "seq"), axis=1, tiled=True).astype(
            part_qkv.dtype
        ),
        lax.all_gather(part_proj.astype(jnp.bfloat16), ("dp", "seq"), axis=1, tiled=True).astype(
            part_proj.dtype
        ),
        lax.all_gather(part_expert.astype(jnp.bfloat16), ("dp", "seq"), axis=2, tiled=True).astype(
            part_expert.dtype
        ),
    )
    summed_route, summed_gains = lax.psum((shard_route, shard_gains), ("dp", "seq"))
    return (
        block_out.astype(jnp.bfloat16)[None],
        grad_x.astype(jnp.bfloat16)[None],
        summed_qkv,
        summed_proj,
        summed_route,
        summed_gains,
        summed_expert,
    )


def solution(mesh):
    in_specs = (
        P(("dp", "fsdp"), "seq", None),
        P("fsdp", None),
        P("fsdp", None),
        P("fsdp", None),
        P("fsdp", None),
        P("fsdp", None, None),
        P(("dp", "fsdp"), "seq", None),
        P(("dp", "fsdp"), None),
        P(("dp", "fsdp"), "seq", None),
    )
    out_specs = (
        P(("dp", "fsdp"), "seq", None),
        P(("dp", "fsdp"), "seq", None),
        P("fsdp", None),
        P("fsdp", None),
        P("fsdp", None),
        P("fsdp", None),
        P("fsdp", None, None),
    )
    return jax.shard_map(shards, mesh=mesh, in_specs=in_specs, out_specs=out_specs, check_vma=False)
```

profile of v0, /device:TPU:9, one launch (start us, length us, event | category | flops | bytes accessed | tf_op | source)
XLA Modules:
  0.0 1858.4 jit_solution(3492848803113367879)
XLA Ops:
  27.7 50.6 %all-gather.7.cloned.1.call-done = bf16[768,2304]{1,0:T(8,128)(2,1)} async-done(((bf16[192,2304]{1,0:T(8,128)(2,1)}), bf16[768,2304]{1,0:T(8,128)(2,1)}) %all-gather.7.cloned.1.call-update) | async-done | bytes 3538960 | tf_op jit(solution)/shard_map/all_gather | solution.py:73
  151.0 65.0 %while.28 = (s32[]{:T(128)}, bf16[3,512,6,64]{1,3,2,0:T(8,128)(2,1)}, f32[3,6,512]{2,1,0:T(8,128)}, s32[3]{0:T(128)S(1)}, s32[1536]{0:T(1024)S(1)}, /*index=5*/b...) while((s32[]{:T(128)}, ...), condition=%wide.region_4.5_spmd.clone, body=%wide.region_1.4_spmd.clone.sunk | while | flops 1267923968 | bytes 63042744 | solution.py:125
  294.8 445.3 %all-gather.11.cloned.1.call-done = bf16[3072,4,1536]{2,0,1:T(8,128)(2,1)} async-done(((bf16[768,4,1536]{2,0,1:T(8,128)(2,1)}), bf16[3072,4,1536]{2,0,1:T(8,128)(2,1)}) %all-gather.11.cloned.1.call-update) | async-done | bytes 37748752 | tf_op jit(solution)/shard_map/all_gather | solution.py:146
  740.2 18.9 %fusion.56 = f32[4,384,3072]{2,1,0:T(8,128)} fusion(bf16[3072,4,1536]{2,0,1:T(8,128)(2,1)} %all-gather.11.cloned.1.call-done, bf16[4,384,768]{1,2,0:T(8,128)(2,1)S(1)} %copy-done.23, pred[4,384]{1,0:T(4,128)(4,1)S(1)} %copy-done.63), kind=kOutput, calls=%fused_computation.77 | convolution fusion | flops 7248936960 | bytes 40109568 | tf_op jit(solution)/shard_map/ecd,fed->ecf/dot_general | solution.py:42
  759.0 19.1 %convert_bitcast_fusion = bf16[3072,4,768]{0,2,1:T(8,128)(2,1)} fusion(bf16[4,384,768]{1,2,0:T(8,128)(2,1)S(1)} %copy-done.25, pred[4,384]{1,0:T(4,128)(4,1)S(1)} %copy-done.63, f32[4,384,3072]{2,1,0:T(8,128)} %fusion.56), kind=kOutput, calls=%fused_computation.68 | convolution fusion | flops 7300841472 | bytes 40109568 | tf_op jit(solution)/shard_map/ecf,ecd->fed/dot_general | solution.py:176
  778.1 25.0 %fusion.49 = bf16[4,384,3072]{2,1,0:T(8,128)(2,1)} fusion(f32[4,384,3072]{2,1,0:T(8,128)} %fusion.56, bf16[3072,4,1536]{2,0,1:T(8,128)(2,1)} %all-gather.11.cloned.1.call-done, bf16[4,384,768]{1,2,0:T(8,128)(2,1)} %copy.335, pred[4,384]{1,0:T(4,128)(4,1)S(1)} %copy-done.63), kind=kOutput, calls=%fused_computation.67 | convolution fusion | flops 7343308800 | bytes 49546752 | tf_op jit(solution)/shard_map/ecd,fed->ecf/dot_general | solution.py:56
  803.1 17.0 convert_bitcast_fusion.1
  820.1 25.8 %pad_maximum_fusion = bf16[3072,4,1536]{0,2,1:T(8,128)(2,1)} fusion(bf16[3072,4,768]{0,2,1:T(8,128)(2,1)} %convert_bitcast_fusion, bf16[3072,4,768]{0,2,1:T(8,128)(2,1)} %convert_bitcast_fusion.1), kind=kLoop, calls=%fused_computation.58 | loop fusion | flops 75497472 | bytes 75497472 | tf_op jit(solution)/shard_map/concatenate | solution.py:180
  847.4 19.3 %fusion.52 = f32[4,384,768]{2,1,0:T(8,128)} fusion(bf16[3072,4,1536]{2,0,1:T(8,128)(2,1)} %all-gather.11.cloned.1.call-done, f32[4,384,3072]{2,1,0:T(8,128)} %fusion.56), kind=kOutput, calls=%fused_computation.73 | convolution fusion | flops 7290224640 | bytes 42467328 | tf_op jit(solution)/shard_map/ecf,fed->ecd/dot_general | solution.py:49
  904.4 16.9 fusion.54
  989.6 176.0 %while.29 = (s32[]{:T(128)}, f32[1536,6,64]{0,2,1:T(8,128)S(1)}, f32[1536,6,64]{0,2,1:T(8,128)}, bf16[3,512,6,64]{1,3,2,0:T(8,128)(2,1)}, s32[3]{0:T(128)S(1)}, ...) while((s32[]{:T(128)}, f32[1536,6,64]{0,2,1:T(8,128)S(1)}, ...), condition=%wide.region_22.23_spmd.clone, body=%wide.region_20.22_spmd.clone.sunk | while | flops 3096968192 | bytes 245085472 | solution.py:237
  1189.6 49.2 %all-to-all-done.3 = bf16[1536,3,1,384]{3,1,2,0:T(4,128)(2,1)} async-done(((bf16[1536,3,1,384]{3,1,2,0:T(4,128)(2,1)}), bf16[1536,3,1,384]{3,1,2,0:T(4,128)(2,1)}, u32[]{:S(2)}, u32[]{:S(2)}) %all-to-all-start.3) | async-done | bytes 3538976 | tf_op jit(solution)/shard_map/all_to_all | solution.py:249
  1252.8 210.5 %reduce-scatter.21.cloned.1.call-done = bf16[768,4,1536]{0,2,1:T(8,128)(2,1)} async-done(((bf16[3072,4,1536]{0,2,1:T(8,128)(2,1)}), bf16[768,4,1536]{0,2,1:T(8,128)(2,1)}) %reduce-scatter.21.cloned.1.call-update) | async-done | bytes 9437200 | tf_op jit(solution)/shard_map/reduce_scatter | solution.py:179
  1475.0 22.5 %reduce-scatter.19.cloned.1.call-done = bf16[192,768]{1,0:T(8,128)(2,1)} async-done(((bf16[768,768]{1,0:T(8,128)(2,1)}), bf16[192,768]{1,0:T(8,128)(2,1)}) %reduce-scatter.19.cloned.1.call-update) | async-done | bytes 294928 | tf_op jit(solution)/shard_map/reduce_scatter | solution.py:263
  1499.4 67.3 %reduce-scatter.17.cloned.1.call-done = bf16[192,2304]{1,0:T(8,128)(2,1)} async-done(((bf16[768,2304]{1,0:T(8,128)(2,1)}), bf16[192,2304]{1,0:T(8,128)(2,1)}) %reduce-scatter.17.cloned.1.call-update) | async-done | bytes 884752 | tf_op jit(solution)/shard_map/reduce_scatter | solution.py:260
  1569.1 78.5 %reduce-scatter.23.cloned.1.call-done = bf16[768,4,192]{0,2,1:T(8,128)(2,1)} async-done(((bf16[768,4,1536]{0,2,1:T(8,128)(2,1)}), bf16[768,4,192]{0,2,1:T(8,128)(2,1)}) %reduce-scatter.23.cloned.1.call-update) | async-done | bytes 1179664 | tf_op jit(solution)/shard_map/reduce_scatter | solution.py:280
  1649.1 15.6 reduce-scatter.29.cloned.1.call-done
  1686.0 16.4 all-reduce.3
  1702.4 22.7 %reduce-scatter.27.cloned.1.call-done = bf16[96,192]{1,0:T(8,128)(2,1)} async-done(((bf16[768,192]{1,0:T(8,128)(2,1)}), bf16[96,192]{1,0:T(8,128)(2,1)}) %reduce-scatter.27.cloned.1.call-update) | async-done | bytes 36880
  1725.1 18.0 all_gather.31
  1744.0 22.4 %reduce-scatter.25.cloned.1.call-done = bf16[288,192]{1,0:T(8,128)(2,1)} async-done(((bf16[2304,192]{1,0:T(8,128)(2,1)}), bf16[288,192]{1,0:T(8,128)(2,1)}) %reduce-scatter.25.cloned.1.call-update) | async-done | bytes 110608
  1766.4 28.3 %all_gather.30 = bf16[192,2304]{0,1:T(8,128)(2,1)S(1)} all-gather(bf16[192,288]{0,1:T(8,128)(2,1)} %bitcast.212), channel_id=1, replica_groups=mesh['dp'=4,'seq'=2,'fsdp'=4] {'dp','seq'}, dimensions={1}, use_global_device_ids=true | all-gather | bytes 995328 | tf_op jit(solution)/shard_map/all_gather | solution.py:285
  1796.2 37.4 %all-gather.13.cloned.1.call-done = bf16[768,4,1536]{0,2,1:T(8,128)(2,1)} async-done(((bf16[768,4,192]{0,2,1:T(8,128)(2,1)}), bf16[768,4,1536]{0,2,1:T(8,128)(2,1)}) %all-gather.13.cloned.1.call-update) | async-done | bytes 9437200 | tf_op jit(solution)/shard_map/all_gather | solution.py:291
  1833.6 17.8 copy.352
  (372 shorter events, 586.1 us)
Async XLA Ops:
  7.2 71.2 %all-gather.7.cloned.1.call-start = ((), (), s32[]{:S(2)}) async-start(), calls=%async_computation.12 | async-start | bytes 4423680 | tf_op jit(solution)/shard_map/all_gather | solution.py:73
  7.9 257.4 %all-gather.9.cloned.1.call-start = ((), (), s32[]{:S(2)}) async-start(), calls=%async_computation.13 | async-start | bytes 1474560 | tf_op jit(solution)/shard_map/all_gather | solution.py:74
  8.6 731.5 %all-gather.11.cloned.1.call-start = ((), (), s32[]{:S(2)}) async-start(), calls=%async_computation.14 | async-start | bytes 47185920 | tf_op jit(solution)/shard_map/all_gather | solution.py:146
  26.7 51.6 %copy-start.12 = (bf16[1,768,768]{1,2,0:T(8,128)(2,1)}, bf16[1,768,768]{1,2,0:T(8,128)(2,1)S(1)}, u32[]{:S(2)}) copy-start(bf16[1,768,768]{1,2,0:T(8,128)(2,1)S(1)} %copy.309) | copy-start | bytes 3538948
  27.4 50.9 %copy-start.58 = (f32[768]{0:T(1024)}, f32[768]{0:T(1024)S(1)}, u32[]{:S(2)}) copy-start(f32[768]{0:T(1024)S(1)} %get-tuple-element.269) | copy-start | bytes 9220
  27.7 50.6 %copy-start.60 = (f32[768]{0:T(1024)}, f32[768]{0:T(1024)S(1)}, u32[]{:S(2)}) copy-start(f32[768]{0:T(1024)S(1)} %add_rsqrt_fusion.1) | copy-start | bytes 9220
  93.6 50.6 %all-to-all-start = ((bf16[768,3,2,384]{3,0,1,2:T(8,128)(2,1)}), bf16[768,3,2,384]{3,0,1,2:T(8,128)(2,1)S(1)}, u32[]{:S(2)}, u32[]{:S(2)}) async-start(bf16[768,3,2,384]{3,0,1,2:T(8,128)(2,1)} %copy.311), calls=%async_computation | async-start | bytes 7077888 | tf_op jit(solution)/shard_map/all_to_all | solution.py:85
  124.5 20.1 %copy-start.56 = (s32[1536]{0:T(1024)}, s32[1536]{0:T(1024)S(1)}, u32[]{:S(2)}) copy-start(s32[1536]{0:T(1024)S(1)} %fusion.98) | copy-start | bytes 18436
  241.4 19.0 %all-to-all-start.1 = ((bf16[2,2,147456]{2,1,0:T(2,128)(2,1)}), bf16[2,2,147456]{2,1,0:T(2,128)(2,1)}, u32[]{:S(2)}, u32[]{:S(2)}) async-start(bf16[2,2,147456]{2,1,0:T(2,128)(2,1)} %reshape.523), calls=%async_computation.1 | async-start | bytes 2359296 | tf_op jit(solution)/shard_map/all_to_all | solution.py:127
  245.8 1217.4 %reduce-scatter.21.cloned.1.call-start = ((), (), s32[]{:S(2)}) async-start(), calls=%async_computation.17 | async-start | bytes 47185920 | tf_op jit(solution)/shard_map/reduce_scatter | solution.py:179
  290.4 449.8 %copy-start.23 = (bf16[4,384,768]{1,2,0:T(8,128)(2,1)S(1)}, bf16[4,384,768]{1,2,0:T(8,128)(2,1)}, u32[]{:S(2)}) copy-start(bf16[4,384,768]{1,2,0:T(8,128)(2,1)} %copy.326) | copy-start | bytes 7077892
  290.4 449.8 %copy-start.63 = (pred[4,384]{1,0:T(4,128)(4,1)S(1)}, pred[4,384]{1,0:T(4,128)(4,1)}, u32[]{:S(2)}) copy-start(pred[4,384]{1,0:T(4,128)(4,1)} %gt.8) | copy-start | bytes 4612
  740.2 18.9 %copy-start.25 = (bf16[4,384,768]{1,2,0:T(8,128)(2,1)S(1)}, bf16[4,384,768]{1,2,0:T(8,128)(2,1)}, u32[]{:S(2)}) copy-start(bf16[4,384,768]{1,2,0:T(8,128)(2,1)} %copy.335) | copy-start | bytes 7077892
  963.0 18.2 all-to-all-start.2
  1181.3 57.6 %all-to-all-start.3 = ((bf16[1536,3,1,384]{3,1,2,0:T(4,128)(2,1)}), bf16[1536,3,1,384]{3,1,2,0:T(4,128)(2,1)}, u32[]{:S(2)}, u32[]{:S(2)}) async-start(bf16[1536,3,1,384]{3,1,2,0:T(4,128)(2,1)} %copy.341), calls=%async_computation.3 | async-start | bytes 9437184 | tf_op jit(solution)/shard_map/all_to_all | solution.py:249
  1187.3 310.2 %reduce-scatter.19.cloned.1.call-start = ((), (), s32[]{:S(2)}) async-start(), calls=%async_computation.16 | async-start | bytes 1474560 | tf_op jit(solution)/shard_map/reduce_scatter | solution.py:263
  1189.6 377.2 %reduce-scatter.17.cloned.1.call-start = ((), (), s32[]{:S(2)}) async-start(), calls=%async_computation.15 | async-start | bytes 4423680 | tf_op jit(solution)/shard_map/reduce_scatter | solution.py:260
  1252.7 394.9 %reduce-scatter.23.cloned.1.call-start = ((), (), s32[]{:S(2)}) async-start(), calls=%async_computation.18 | async-start | bytes 10616832 | tf_op jit(solution)/shard_map/reduce_scatter | solution.py:280
  1463.3 201.4 %reduce-scatter.29.cloned.1.call-start = ((), (), s32[]{:S(2)}) async-start(), calls=%async_computation.22 | async-start | bytes 245760
  1466.5 218.6 %reduce-scatter.31.cloned.1.call-start = ((), (), s32[]{:S(2)}) async-start(), calls=%async_computation.23 | async-start | bytes 245760
  1475.0 250.1 %reduce-scatter.27.cloned.1.call-start = ((), (), s32[]{:S(2)}) async-start(), calls=%async_computation.21 | async-start | bytes 442368
  1499.4 148.3 %copy-start.18 = (bf16[1,768,768]{1,2,0:T(8,128)(2,1)S(1)}, bf16[1,768,768]{1,2,0:T(8,128)(2,1)}, u32[]{:S(2)}) copy-start(bf16[1,768,768]{1,2,0:T(8,128)(2,1)} %get-tuple-element.320) | copy-start | bytes 3538948
  1499.4 267.0 %reduce-scatter.25.cloned.1.call-start = ((), (), s32[]{:S(2)}) async-start(), calls=%async_computation.20 | async-start | bytes 1327104
  1569.1 264.5 %all-gather.13.cloned.1.call-start = ((), (), s32[]{:S(2)}) async-start(), calls=%async_computation.19 | async-start | bytes 10616832 | tf_op jit(solution)/shard_map/all_gather | solution.py:291
  (66 other events, 292.7 us)
Sparse Core Ops, SparseCore 0:
  9.6 68.7 all-gather.6
  79.9 30.8 all-gather.8
  112.9 627.1 all-gather.10
  846.1 617.1 reduce-scatter.20
  1466.1 31.3 reduce-scatter.18
  1499.8 66.9 reduce-scatter.16
  1570.6 76.9 reduce-scatter.22
  1649.9 14.7 reduce-scatter.28
  1667.5 17.5 reduce-scatter.30
  1688.9 36.0 reduce-scatter.26
  1729.2 37.1 reduce-scatter.24
  1768.2 65.3 all-gather.12
where the time goes:
time: 1870 us; the launch traced here: 1860 us
  waiting for transfers between devices  1050 us (56%)
  matrix products  285 us (15%)
  local copies, waits for them, and re-layouts  250 us (13%)
  other arithmetic  143 us (8%)
  blocking collectives  80.1 us (4%)
  starting transfers between devices  18.8 us (1%)
    all_gather x1, waiting for transfers between devices, shards(): piece = lax.all_gather(expert_w, 'fsdp', axis=0, tiled=True)  445 us
    reduce_scatter x1, waiting for transfers between devices, shards(): lax.psum_scatter(jnp.concatenate([grad_first, grad_second], axis=2).astyp...  211 us
    reduce_scatter x1, waiting for transfers between devices, shards(): lax.psum_scatter(expert_shard, ('dp', 'seq'), scatter_dimension=2, tiled=...  78.5 us
    unnamed x16, waiting for transfers between devices  77.3 us
    reduce_scatter x1, waiting for transfers between devices, shards(): lax.psum_scatter(grad_qkv_w.astype(jnp.bfloat16), 'fsdp', scatter_dimensi...  67.3 us
    unnamed x149, local copies, waits for them, and re-layouts  58 us
    all_gather x1, waiting for transfers between devices, shards(): lax.all_gather(attn_in, 'fsdp', axis=0, tiled=True)  50.6 us
    all_to_all x1, waiting for transfers between devices, shards(): lax.all_to_all(stacked, 'seq', split_axis=0, concat_axis=2, tiled=True)  49.2 us
  transfers between devices with their start and end apart: 16, of which 13 were waited for; matrix products, arithmetic and copies ran while one was open for 28% of the time, Pallas kernels for 0%

commit v1 on v0

v1 whole, which is shorter than its diff:
```python
import functools

import jax
import jax.numpy as jnp
from jax import lax
from jax.experimental import pallas as pl
from jax.experimental.pallas import tpu as pltpu
from jax.sharding import PartitionSpec as P

HEADS = 12
HEAD_DIM = 64
EXPERTS = 4
EPSILON = 1e-06
NEGATIVE = -1e30
LOG2E = 1.4426950408889634
BF = jnp.bfloat16
F32 = jnp.float32
MESH = pl.DeviceIdType.MESH
VMEM_LIMIT = 60 << 20
QB = 256
ANY = pl.BlockSpec(memory_space=pl.ANY)
VM = pl.BlockSpec(memory_space=pltpu.VMEM)


def nn(a, b):
    return lax.dot_general(a, b, (((1,), (0,)), ((), ())), preferred_element_type=F32)


def nt(a, b):
    return lax.dot_general(a, b, (((1,), (1,)), ((), ())), preferred_element_type=F32)


def tn(a, b):
    return lax.dot_general(a, b, (((0,), (0,)), ((), ())), preferred_element_type=F32)


def iota(shape, dim):
    return lax.broadcasted_iota(jnp.int32, shape, dim)


def params(cid=None):
    if cid is None:
        return pltpu.CompilerParams(vmem_limit_bytes=VMEM_LIMIT)
    return pltpu.CompilerParams(
        vmem_limit_bytes=VMEM_LIMIT, collective_id=cid, has_side_effects=True
    )


def sds(shape, dtype):
    return jax.ShapeDtypeStruct(shape, dtype)


def place():
    dp, sq, z = lax.axis_index("dp"), lax.axis_index("seq"), lax.axis_index("fsdp")
    return dp, sq, z, dp // 2, lax.rem(dp, 2)


def greet(peers):
    barrier = pltpu.get_barrier_semaphore()
    for peer in peers:
        pl.semaphore_signal(barrier, inc=1, device_id=peer, device_id_type=MESH)
    pl.semaphore_wait(barrier, len(peers))


def remote(src, dst, send, recv, peer):
    return pltpu.make_async_remote_copy(
        src_ref=src, dst_ref=dst, send_sem=send, recv_sem=recv, device_id=peer, device_id_type=MESH
    )


def al(x):
    return pl.multiple_of(x, 128)


def heads_in_kernel(parts, src, dst, local, send, recv):
    dp, sq, z, _, _ = place()
    rows, half = src.shape[0], src.shape[1] // parts // 2
    peer = (dp, 1 - sq, z)
    greet([peer])
    mine = pl.ds(pl.multiple_of(sq * rows, rows), rows)
    copies = []
    for i in range(parts):
        out = dst.at[mine, pl.ds(i * half, half)]
        theirs = src.at[:, pl.ds(al((2 * i + 1 - sq) * half), half)]
        own = src.at[:, pl.ds(al((2 * i + sq) * half), half)]
        copies.append(remote(theirs, out, send.at[i], recv.at[i], peer))
        copies.append(pltpu.make_async_copy(own, out, local.at[i]))
    for c in copies:
        c.start()
    for c in copies:
        c.wait()


def heads_in(x, parts, cid):
    rows, cols = x.shape
    return pl.pallas_call(
        functools.partial(heads_in_kernel, parts),
        out_shape=sds((2 * rows, cols // 2), x.dtype),
        in_specs=[ANY],
        out_specs=ANY,
        scratch_shapes=[pltpu.SemaphoreType.DMA((parts,))] * 3,
        compiler_params=params(cid),
        name=f"heads_in_{parts}",
    )(x)


def heads_out_kernel(parts, *refs):
    srcs, dst, local, send, recv = refs[:parts], refs[parts], *refs[parts + 1 :]
    dp, sq, z, _, _ = place()
    rows, half = dst.shape[0], srcs[0].shape[1]
    peer = (dp, 1 - sq, z)
    greet([peer])
    copies = []
    for i in range(parts):
        out = dst.at[:, pl.ds(al((2 * i + sq) * half), half)]
        theirs = srcs[i].at[pl.ds(pl.multiple_of((1 - sq) * rows, rows), rows)]
        own = srcs[i].at[pl.ds(pl.multiple_of(sq * rows, rows), rows)]
        copies.append(remote(theirs, out, send.at[i], recv.at[i], peer))
        copies.append(pltpu.make_async_copy(own, out, local.at[i]))
    for c in copies:
        c.start()
    for c in copies:
        c.wait()


def heads_out(xs, cid):
    parts = len(xs)
    rows, half = xs[0].shape
    return pl.pallas_call(
        functools.partial(heads_out_kernel, parts),
        out_shape=sds((rows // 2, parts * 2 * half), xs[0].dtype),
        in_specs=[ANY] * parts,
        out_specs=ANY,
        scratch_shapes=[pltpu.SemaphoreType.DMA((parts,))] * 3,
        compiler_params=params(cid),
        name=f"heads_out_{parts}",
    )(*xs)


def chips_kernel(parts, *refs):
    srcs, dsts = refs[:parts], refs[parts : 2 * parts]
    local, send, recv = refs[2 * parts :]
    dp, sq, z, x, core = place()
    flips = [(1, 0), (0, 1), (1, 1)]

    def chip(fx, fy):
        px = x if fx == 0 else 1 - x
        py = sq if fy == 0 else 1 - sq
        return px * 2 + py, (px * 2 + core, py, z)

    me, _ = chip(0, 0)
    greet([chip(*f)[1] for f in flips])
    copies = []
    for i in range(parts):
        for j, f in enumerate(flips):
            there, peer = chip(*f)
            copies.append(
                remote(srcs[i].at[there], dsts[i].at[me], send.at[i, j], recv.at[i, j], peer)
            )
        copies.append(pltpu.make_async_copy(srcs[i].at[me], dsts[i].at[me], local.at[i]))
    for c in copies:
        c.start()
    for c in copies:
        c.wait()


def chips(xs, cid):
    parts = len(xs)
    return pl.pallas_call(
        functools.partial(chips_kernel, parts),
        out_shape=tuple(sds(x.shape, x.dtype) for x in xs),
        in_specs=[ANY] * parts,
        out_specs=tuple([ANY] * parts),
        scratch_shapes=[
            pltpu.SemaphoreType.DMA((parts,)),
            pltpu.SemaphoreType.DMA((parts, 3)),
            pltpu.SemaphoreType.DMA((parts, 3)),
        ],
        compiler_params=params(cid),
        name=f"chips_{parts}",
    )(*xs)


def cores_join_kernel(src, dst, local, send, recv):
    dp, sq, z, x, core = place()
    peer = (x * 2 + 1 - core, sq, z)
    greet([peer])
    copies = [
        remote(src, dst.at[:, core], send, recv, peer),
        pltpu.make_async_copy(src, dst.at[:, core], local),
    ]
    for c in copies:
        c.start()
    for c in copies:
        c.wait()


def cores_join(x, cid):
    n, r, k = x.shape
    return pl.pallas_call(
        cores_join_kernel,
        out_shape=sds((n, 2, r, k), x.dtype),
        in_specs=[ANY],
        out_specs=ANY,
        scratch_shapes=[pltpu.SemaphoreType.DMA(())] * 3,
        compiler_params=params(cid),
        name="cores_join",
    )(x)


def cores_sum_kernel(src, dst, got, own, sem, send, recv):
    dp, sq, z, x, core = place()
    peer = (x * 2 + 1 - core, sq, z)
    greet([peer])
    n = src.shape[0]
    there = [remote(src.at[i, 1 - core], got.at[i], send.at[i], recv.at[i], peer) for i in range(n)]
    here = pltpu.make_async_copy(src.at[:, core], own, sem)
    for c in there:
        c.start()
    here.start()
    here.wait()
    for i in range(n):
        there[i].wait()
        dst[i] = (own[i].astype(F32) + got[i].astype(F32)).astype(BF)


def cores_sum(x, cid):
    n, _, r, k = x.shape
    return pl.pallas_call(
        cores_sum_kernel,
        out_shape=sds((n, r, k), x.dtype),
        in_specs=[ANY],
        out_specs=VM,
        scratch_shapes=[
            pltpu.VMEM((n, r, k), x.dtype),
            pltpu.VMEM((n, r, k), x.dtype),
            pltpu.SemaphoreType.DMA(()),
            pltpu.SemaphoreType.DMA((n,)),
            pltpu.SemaphoreType.DMA((n,)),
        ],
        compiler_params=params(cid),
        name="cores_sum",
    )(x)


def front_kernel(x_ref, gain_ref, w_ref, proj_ref):
    x = x_ref[...].astype(F32)
    r_one = lax.rsqrt(jnp.mean(x * x, axis=1, keepdims=True) + EPSILON)
    normed = (x * r_one * gain_ref[...]).astype(BF)
    cols = 768
    for j in range(0, w_ref.shape[1], cols):
        proj_ref[:, j : j + cols] = nn(normed, w_ref[:, j : j + cols]).astype(BF)


def front(x, gain, w):
    return pl.pallas_call(
        front_kernel,
        out_shape=sds((x.shape[0], w.shape[1]), BF),
        in_specs=[VM] * 3,
        out_specs=VM,
        compiler_params=params(),
        name="front",
    )(x, gain, w)


def allowed_tile(j, i, prompt, seg_col, seg_row):
    mask = None
    if i == j:
        mask = iota((QB, QB), 0) <= iota((QB, QB), 1)
    if (j + 1) * QB > prompt:
        segs = seg_col[j * QB : (j + 1) * QB, :]
        same = segs == seg_row[:, i * QB : (i + 1) * QB]
        if j * QB < prompt:
            same = same | (segs < 0)
        mask = same if mask is None else mask & same
    return mask


def attend_kernel(prompt, seg_row, seg_col, q_ref, k_ref, v_ref, o_ref, lse_ref, vt):
    half = lax.rem(pl.program_id(0), 2)
    blocks = q_ref.shape[0] // QB
    width = q_ref.shape[1]
    lanes = iota((1, width), 1) // HEAD_DIM == half
    const = HEAD_DIM ** (-0.5) * LOG2E
    vt[0:width, :] = v_ref[...].T
    vt[width : width + 16, :] = jnp.ones((16, vt.shape[1]), BF)
    for i in range(blocks):
        rows = slice(i * QB, (i + 1) * QB)
        q = jnp.where(lanes, q_ref[rows, :], jnp.zeros((), BF))
        tiles = []
        for j in range(i + 1):
            s = nt(k_ref[j * QB : (j + 1) * QB, :], q)
            mask = allowed_tile(j, i, prompt, seg_col, seg_row)
            if mask is not None:
                s = jnp.where(mask, s, NEGATIVE)
            tiles.append(s)
        top = functools.reduce(jnp.maximum, [jnp.max(s, axis=0, keepdims=True) for s in tiles])
        top = top * const
        acc = None
        for j, s in enumerate(tiles):
            p = jnp.exp2(s * const - top).astype(BF)
            part = nn(vt[:, j * QB : (j + 1) * QB], p)
            acc = part if acc is None else acc + part
        total = acc[width : width + 1, :]
        lse_ref[0, 0:1, rows] = top + jnp.log2(total)
        out = (acc[0:width, :] * (1.0 / total)).T.astype(BF)
        o_ref[rows, :] = jnp.where(lanes, out, o_ref[rows, :])


def attend(qkv, seg_row, seg_col, prompt):
    group, cols = qkv.shape
    pairs = cols // 3 // 128
    return pl.pallas_call(
        functools.partial(attend_kernel, prompt),
        grid=(2 * pairs,),
        out_shape=(sds((group, cols // 3), BF), sds((2 * pairs, 8, group), F32)),
        in_specs=[
            pl.BlockSpec((1, group), lambda h: (0, 0)),
            pl.BlockSpec((group, 1), lambda h: (0, 0)),
            pl.BlockSpec((group, 128), lambda h: (0, h // 2)),
            pl.BlockSpec((group, 128), lambda h: (0, pairs + h // 2)),
            pl.BlockSpec((group, 128), lambda h: (0, 2 * pairs + h // 2)),
        ],
        out_specs=(
            pl.BlockSpec((group, 128), lambda h: (0, h // 2)),
            pl.BlockSpec((1, 8, group), lambda h: (h, 0, 0)),
        ),
        scratch_shapes=[pltpu.VMEM((128 + 16, group), BF)],
        compiler_params=params(),
        name="attend",
    )(seg_row, seg_col, qkv, qkv, qkv)


def attend_back_kernel(
    prompt, seg_row, seg_col, q_ref, k_ref, v_ref, o_ref, lse_ref, do_ref, dq_ref, dk_ref, dv_ref,
    qm, dom, kt, dqt,
):
    half = lax.rem(pl.program_id(0), 2)
    blocks = q_ref.shape[0] // QB
    width = q_ref.shape[1]
    lanes = iota((1, width), 1) // HEAD_DIM == half
    scale = HEAD_DIM ** (-0.5)
    zero = jnp.zeros((), BF)
    qm[...] = jnp.where(lanes, q_ref[...], zero) * jnp.asarray(scale, BF)
    dom[...] = jnp.where(lanes, do_ref[...], zero)
    kt[...] = k_ref[...].T
    prod = (dom[...].astype(F32) * o_ref[...].astype(F32)).T
    delta = jnp.sum(prod, axis=0, keepdims=True)
    lse = lse_ref[0, 0:1, :]
    for j in range(blocks):
        keys = slice(j * QB, (j + 1) * QB)
        k, v = k_ref[keys, :], v_ref[keys, :]
        dk = dv = None
        for i in range(j, blocks):
            rows = slice(i * QB, (i + 1) * QB)
            s = nt(k, qm[rows, :])
            dp = nt(v, dom[rows, :])
            p = jnp.exp2(s * LOG2E - lse[:, rows])
            mask = allowed_tile(j, i, prompt, seg_col, seg_row)
            if mask is not None:
                p = jnp.where(mask, p, 0.0)
            ds = (p * (dp - delta[:, rows])).astype(BF)
            a = nn(p.astype(BF), dom[rows, :])
            b = nn(ds, qm[rows, :])
            c = nn(kt[:, keys], ds)
            dv = a if dv is None else dv + a
            dk = b if dk is None else dk + b
            dqt[:, rows] = c if j == 0 else dqt[:, rows] + c
        dk_ref[keys, :] = jnp.where(lanes, dk.astype(BF), dk_ref[keys, :])
        dv_ref[keys, :] = jnp.where(lanes, dv.astype(BF), dv_ref[keys, :])
    dq = (dqt[...] * scale).T.astype(BF)
    dq_ref[...] = jnp.where(lanes, dq, dq_ref[...])


def attend_back(qkv, seg_row, seg_col, out, lse, grad, prompt):
    group, cols = qkv.shape
    pairs = cols // 3 // 128
    pair = pl.BlockSpec((group, 128), lambda h: (0, h // 2))
    return pl.pallas_call(
        functools.partial(attend_back_kernel, prompt),
        grid=(2 * pairs,),
        out_shape=tuple([sds((group, cols // 3), BF)] * 3),
        in_specs=[
            pl.BlockSpec((1, group), lambda h: (0, 0)),
            pl.BlockSpec((group, 1), lambda h: (0, 0)),
            pair,
            pl.BlockSpec((group, 128), lambda h: (0, pairs + h // 2)),
            pl.BlockSpec((group, 128), lambda h: (0, 2 * pairs + h // 2)),
            pair,
            pl.BlockSpec((1, 8, group), lambda h: (h, 0, 0)),
            pair,
        ],
        out_specs=(pair, pair, pair),
        scratch_shapes=[
            pltpu.VMEM((group, 128), BF),
            pltpu.VMEM((group, 128), BF),
            pltpu.VMEM((128, group), BF),
            pltpu.VMEM((128, group), F32),
        ],
        compiler_params=params(),
        name="attend_back",
    )(seg_row, seg_col, qkv, qkv, qkv, out, lse, grad)


def slot_rows(places_row, e, capacity):
    rows = places_row[e : e + 1, :]
    return (rows == iota((capacity, 1), 0).astype(F32)).astype(F32).astype(BF)


def slot_cols(places_col, e, capacity):
    cols = places_col[:, e : e + 1]
    return (cols == iota((1, capacity), 1).astype(F32)).astype(F32).astype(BF)


def take_kernel(capacity, places_row, rows_ref, out_ref):
    for e in range(EXPERTS):
        out_ref[e] = nn(slot_rows(places_row, e, capacity), rows_ref[...]).astype(BF)


def take(places_row, rows, capacity):
    return pl.pallas_call(
        functools.partial(take_kernel, capacity),
        out_shape=sds((EXPERTS, capacity, rows.shape[1]), BF),
        in_specs=[VM] * 2,
        out_specs=VM,
        compiler_params=params(),
        name="take",
    )(places_row, rows)


def softmax_lanes(logits):
    live = iota(logits.shape, 1) < EXPERTS
    logits = jnp.where(live, logits, NEGATIVE)
    expo = jnp.where(live, jnp.exp(logits - jnp.max(logits, axis=1, keepdims=True)), 0.0)
    return expo / jnp.sum(expo, axis=1, keepdims=True)


def middle_kernel(
    capacity, x_ref, att_ref, w_ref, gain_ref, router_ref, places_row, places_col,
    hidden_ref, probs_ref, in_ref, gate_ref,
):
    hidden = x_ref[...].astype(F32) + nn(att_ref[...], w_ref[...])
    hidden_ref[...] = hidden
    r_two = lax.rsqrt(jnp.mean(hidden * hidden, axis=1, keepdims=True) + EPSILON)
    routed = (hidden * r_two * gain_ref[...]).astype(BF)
    probs = softmax_lanes(nn(routed, router_ref[...]))
    probs_ref[...] = probs
    flat = probs.T[0:8, :]
    high = flat.astype(BF)
    rest = flat - high.astype(F32)
    mid = rest.astype(BF)
    low = (rest - mid.astype(F32)).astype(BF)
    split = jnp.concatenate([high.astype(F32), mid.astype(F32), low.astype(F32)], axis=0).astype(BF)
    for e in range(EXPERTS):
        in_ref[e] = nn(slot_rows(places_row, e, capacity), routed).astype(BF)
        three = nn(split, slot_cols(places_col, e, capacity))
        gate = three[0:8] + three[8:16] + three[16:24]
        gate_ref[e] = jnp.broadcast_to(gate[e : e + 1, :], gate.shape)


def middle(x, attended, w_proj, gain, router, places_row, places_col, capacity):
    rows, width = x.shape
    return pl.pallas_call(
        functools.partial(middle_kernel, capacity),
        out_shape=(
            sds((rows, width), F32),
            sds((rows, 128), F32),
            sds((EXPERTS, capacity, width), BF),
            sds((EXPERTS, 8, capacity), F32),
        ),
        in_specs=[VM] * 7,
        out_specs=(VM,) * 4,
        compiler_params=params(),
        name="middle",
    )(x, attended, w_proj, gain, router, places_row, places_col)


def expert_kernel(
    in_ref, raw_ref, gate_ref, w_ref, res_ref, gin_ref, dot_ref, dw_ref, grad, res_acc, gin_acc
):
    step = pl.program_id(0)
    sources, slots, width = in_ref.shape
    flat = sources * slots

    @pl.when(step == 0)
    def _():
        for i in range(sources):
            gate = gate_ref[i].T[:, 0:1]
            grad[i * slots : (i + 1) * slots, :] = (raw_ref[i].astype(F32) * gate).astype(BF)

    first, second = w_ref[:, :width], w_ref[:, width:]
    x = in_ref[...].reshape(flat, width)
    g = grad[...]
    pre = nt(x, first)
    back = nt(g, second)
    a, b = 0.7978845608028654, 0.7978845608028654 * 0.044715
    square = pre * pre
    t = jnp.tanh(pre * (a + b * square))
    rise = 0.5 + 0.5 * t
    act = (pre * rise).astype(BF)
    slope = rise + (0.5 * pre) * (1.0 - t * t) * (a + (3.0 * b) * square)
    grad_pre = (back * slope).astype(BF)
    res = nn(act, second)
    gin = nn(grad_pre, first)

    @pl.when(step == 0)
    def _():
        res_acc[...] = res
        gin_acc[...] = gin

    @pl.when(step > 0)
    def _():
        res_acc[...] += res
        gin_acc[...] += gin

    dw_ref[:, :width] = tn(grad_pre, x).astype(BF)
    dw_ref[:, width:] = tn(act, g).astype(BF)

    @pl.when(step == pl.num_programs(0) - 1)
    def _():
        for i in range(sources):
            rows = slice(i * slots, (i + 1) * slots)
            res_ref[i] = res_acc[rows, :].astype(BF)
            gin_ref[i] = gin_acc[rows, :].astype(BF)
            prod = res_acc[rows, :] * raw_ref[i].astype(F32)
            narrow = functools.reduce(
                jnp.add, [prod[:, j : j + 128] for j in range(0, width, 128)]
            )
            inner = jnp.sum(narrow.T, axis=0, keepdims=True)
            dot_ref[i] = jnp.broadcast_to(inner, (8, slots))


def expert(expert_in, raw, gate, w, chunk):
    sources, slots, width = expert_in.shape
    hidden = w.shape[0]
    flat = sources * slots
    whole = lambda shape: pl.BlockSpec(shape, lambda s: (0,) * len(shape))
    rows = whole((sources, slots, width))
    small = whole((sources, 8, slots))
    piece = pl.BlockSpec((chunk, 2 * width), lambda s: (s, 0))
    return pl.pallas_call(
        expert_kernel,
        grid=(hidden // chunk,),
        out_shape=(
            sds((sources, slots, width), BF),
            sds((sources, slots, width), BF),
            sds((sources, 8, slots), F32),
            sds((hidden, 2 * width), BF),
        ),
        in_specs=[rows, rows, small, piece],
        out_specs=(rows, rows, small, piece),
        scratch_shapes=[
            pltpu.VMEM((flat, width), BF),
            pltpu.VMEM((flat, width), F32),
            pltpu.VMEM((flat, width), F32),
        ],
        compiler_params=params(),
        name="expert",
    )(expert_in, raw, gate, w)


def after_kernel(
    capacity, res_ref, gin_ref, dot_ref, hidden_ref, probs_ref, places_col, cot_ref, gain_ref,
    router_ref, w_ref, att_ref, out_ref, gh_ref, gatt_ref, dw_ref, dr_ref, dg_ref,
):
    hidden = hidden_ref[...]
    probs = probs_ref[...]
    gain = gain_ref[...]
    lane = iota(probs.shape, 1)
    total = hidden
    back = None
    grad_probs = jnp.zeros_like(probs)
    for e in range(EXPERTS):
        pick = slot_cols(places_col, e, capacity)
        total = total + probs[:, e : e + 1] * nn(pick, res_ref[e])
        part = nn(pick, gin_ref[e])
        back = part if back is None else back + part
        inner = jnp.sum(pick.astype(F32) * dot_ref[e][0:1, :], axis=1, keepdims=True)
        grad_probs = jnp.where(lane == e, inner, grad_probs)
    out_ref[...] = total.astype(BF)
    mixed = jnp.sum(probs * grad_probs, axis=1, keepdims=True)
    grad_logits = probs * (grad_probs - mixed)
    low = grad_logits.astype(BF)
    r_two = lax.rsqrt(jnp.mean(hidden * hidden, axis=1, keepdims=True) + EPSILON)
    h_norm = hidden * r_two
    routed = (h_norm * gain).astype(BF)
    dr_ref[...] = tn(routed, low)
    grad_routed = back + nt(low, router_ref[...])
    dg_ref[...] = jnp.sum(grad_routed * h_norm, axis=0, keepdims=True)
    u = grad_routed * gain
    grad_hidden = cot_ref[...].astype(F32) + r_two * (
        u - h_norm * jnp.mean(u * h_norm, axis=1, keepdims=True)
    )
    gh_ref[...] = grad_hidden
    hid_low = grad_hidden.astype(BF)
    gatt_ref[...] = nt(hid_low, w_ref[...]).astype(BF)
    dw_ref[...] = tn(att_ref[...], hid_low).astype(BF)


def after(res, gin, inner, hidden, probs, places_col, cot, gain, router, w_proj, attended, capacity):
    rows, width = hidden.shape
    return pl.pallas_call(
        functools.partial(after_kernel, capacity),
        out_shape=(
            sds((rows, width), BF),
            sds((rows, width), F32),
            sds((rows, width), BF),
            sds((width, width), BF),
            sds((width, 128), F32),
            sds((1, width), F32),
        ),
        in_specs=[VM] * 11,
        out_specs=(VM,) * 6,
        compiler_params=params(),
        name="after",
    )(res, gin, inner, hidden, probs, places_col, cot, gain, router, w_proj, attended)


def tail_kernel(x_ref, gain_ref, gp_ref, w_ref, gh_ref, dx_ref, dw_ref, dg_ref):
    x = x_ref[...].astype(F32)
    gain = gain_ref[...]
    r_one = lax.rsqrt(jnp.mean(x * x, axis=1, keepdims=True) + EPSILON)
    x_norm = x * r_one
    normed = (x_norm * gain).astype(BF)
    cols = 768
    for j in range(0, gp_ref.shape[1], cols):
        dw_ref[:, j : j + cols] = tn(normed, gp_ref[:, j : j + cols]).astype(BF)
    grad = nt(gp_ref[...], w_ref[...])
    dg_ref[...] = jnp.sum(grad * x_norm, axis=0, keepdims=True)
    u = grad * gain
    dx = gh_ref[...] + r_one * (u - x_norm * jnp.mean(u * x_norm, axis=1, keepdims=True))
    dx_ref[...] = dx.astype(BF)


def tail(x, gain, grad_proj, w_qkv, grad_hidden):
    rows, width = x.shape
    return pl.pallas_call(
        tail_kernel,
        out_shape=(sds((rows, width), BF), sds(w_qkv.shape, BF), sds((1, width), F32)),
        in_specs=[VM] * 5,
        out_specs=(VM,) * 3,
        compiler_params=params(),
        name="tail",
    )(x, gain, grad_proj, w_qkv, grad_hidden)


def shards(tokens, attn_in, attn_out, router, gains, expert_w, expert_ids, segments, cotangent):
    x = tokens[0]
    cot = cotangent[0]
    rows, width = x.shape
    nz = lax.axis_size("fsdp")
    group = 2 * rows
    prompt = group - segments.shape[1]
    capacity = 2 * rows // EXPERTS
    dp, sq = lax.axis_index("dp"), lax.axis_index("seq")
    core = lax.rem(dp, 2)
    mine = (dp // 2) * 2 + sq

    chosen = jnp.sum(
        (expert_ids[0][:, :, None] == jnp.arange(EXPERTS, dtype=jnp.int32)).astype(F32), axis=1
    )
    earlier = (iota((rows, rows), 1) < iota((rows, rows), 0)).astype(BF)
    before = nn(earlier, chosen.astype(BF))
    places = jnp.where(chosen > 0, before, -1.0)
    places_col = jnp.pad(places, ((0, 0), (0, 128 - EXPERTS)), constant_values=-1.0)
    places_row = jnp.pad(places.T, ((0, 8 - EXPERTS), (0, 0)), constant_values=-1.0)
    seg_full = jnp.concatenate([jnp.full((prompt,), -1, jnp.int32), segments[0]])
    seg_row, seg_col = seg_full[None, :], seg_full[:, None]

    packed = jnp.concatenate(
        [attn_in, attn_out, jnp.pad(jnp.concatenate([router, gains], axis=1), ((0, 0), (0, 122)))],
        axis=1,
    )
    whole = lax.all_gather(packed, "fsdp", axis=0, tiled=True)
    w_qkv, w_proj, small = whole[:, : 3 * width], whole[:, 3 * width : 4 * width], whole[:, 4 * width :]
    w_route = jnp.where(jnp.arange(128) < EXPERTS, small, jnp.zeros((), BF))
    gain_rows = small[:, EXPERTS : EXPERTS + 2].astype(F32).T
    gain_one, gain_two = gain_rows[0:1], gain_rows[1:2]
    shard = expert_w.shape[0]
    part = shard // 2
    piece = lax.dynamic_slice(expert_w, (core * part, mine, 0), (part, 1, 2 * width))[:, 0]
    pieces = lax.all_gather(piece, "fsdp", axis=0, tiled=False)

    proj = front(x, gain_one, w_qkv)
    raw = take(places_row, cot, capacity)
    qkv = heads_in(proj, 3, 0)
    mixed, lse = attend(qkv, seg_row, seg_col, prompt)
    attended = heads_out([mixed], 1)
    hidden, probs, expert_in, gate = middle(
        x, attended, w_proj, gain_two, w_route, places_row, places_col, capacity
    )
    there_in, there_raw, there_gate = chips([expert_in, raw, gate], 2)
    w_mine = cores_join(pieces, 3).reshape(nz * shard, 2 * width)
    res, gin, inner, dw = expert(there_in, there_raw, there_gate, w_mine, 512)
    back_res, back_gin, back_inner = chips([res, gin, inner], 4)
    block_out, grad_hidden, grad_att, d_out, d_route, d_gain_two = after(
        back_res, back_gin, back_inner, hidden, probs, places_col, cot, gain_two, w_route, w_proj,
        attended, capacity,
    )
    dw_half = cores_sum(dw.reshape(nz, 2, part, 2 * width), 5)
    dw_own = lax.psum_scatter(
        dw_half.reshape(nz * part, 2 * width), "fsdp", scatter_dimension=0, tiled=True
    )

    grad_mixed = heads_in(grad_att, 1, 6)
    dq, dk, dv = attend_back(qkv, seg_row, seg_col, mixed, lse, grad_mixed, prompt)
    grad_proj = heads_out([dq, dk, dv], 7)
    d_tokens, d_in, d_gain_one = tail(x, gain_one, grad_proj, w_qkv, grad_hidden)

    dw_all = lax.all_gather(dw_own, ("dp", "seq"), axis=0, tiled=False)
    dw_all = dw_all.reshape(2, 2, 2, part, 2 * width).transpose(1, 3, 0, 2, 4)
    d_expert = dw_all.reshape(shard, EXPERTS, 2 * width).astype(F32)

    d_gains = jnp.concatenate([d_gain_one, d_gain_two], axis=0).T
    d_small = jnp.pad(jnp.concatenate([d_route[:, :EXPERTS], d_gains], axis=1), ((0, 0), (0, 122)))
    grads = jnp.concatenate([d_in, d_out, d_small.astype(BF)], axis=1)
    own = lax.psum_scatter(grads, "fsdp", scatter_dimension=0, tiled=True)
    total = lax.psum(own, ("dp", "seq")).astype(F32)
    return (
        block_out[None],
        d_tokens[None],
        total[:, : 3 * width],
        total[:, 3 * width : 4 * width],
        total[:, 4 * width : 4 * width + EXPERTS],
        total[:, 4 * width + EXPERTS : 4 * width + EXPERTS + 2],
        d_expert,
    )


def solution(mesh):
    in_specs = (
        P(("dp", "fsdp"), "seq", None),
        P("fsdp", None),
        P("fsdp", None),
        P("fsdp", None),
        P("fsdp", None),
        P("fsdp", None, None),
        P(("dp", "fsdp"), "seq", None),
        P(("dp", "fsdp"), None),
        P(("dp", "fsdp"), "seq", None),
    )
    out_specs = (
        P(("dp", "fsdp"), "seq", None),
        P(("dp", "fsdp"), "seq", None),
        P("fsdp", None),
        P("fsdp", None),
        P("fsdp", None),
        P("fsdp", None),
        P("fsdp", None, None),
    )
    return jax.shard_map(shards, mesh=mesh, in_specs=in_specs, out_specs=out_specs, check_vma=False)
```

time: 1870 us -> 1050 us (0.56)
  waiting for transfers between devices: 1050 us -> 359 us
  Pallas kernels: 0 us -> 581 us
  matrix products: 285 us -> 0.45 us
  local copies, waits for them, and re-layouts: 250 us -> 70.2 us
  other arithmetic: 143 us -> 10.2 us
  blocking collectives: 80.1 us -> 0 us
    pallas_call x0 -> x16, Pallas kernels: none -> 581 us  [the longest x1 145 us: cores_join(): pl.pallas_call(cores_join_kernel, out_shape=sds((n, 2, r, k), x.dtype), i...]
    all_gather x4 -> x3, waiting for transfers between devices: 533 us -> 133 us  [the longest x1 77.7 us: shards(): pieces = lax.all_gather(piece, 'fsdp', axis=0, tiled=False)]
    dot_general x36 -> x1, matrix products: 285 us -> 0.45 us  [nn(): lax.dot_general(a, b, (((1,), (0,)), ((), ())), preferred_element_type=F32)]
    reduce_scatter x4 -> x2, waiting for transfers between devices: 379 us -> 166 us  [the longest x1 88 us: shards(): lax.psum_scatter(dw_half.reshape(nz * part, 2 * width), 'fsdp', scatter_d...]
    unnamed x16 -> x6, waiting for transfers between devices: 77.3 us -> 0.1 us
    all_to_all x4 -> x0, waiting for transfers between devices: 63.8 us -> none  [the longest x1 49.2 us: shards(): lax.all_to_all(stacked, 'seq', split_axis=0, concat_axis=2, tiled=True)]
    all_gather x4 -> x0, blocking collectives: 63.7 us -> none  [the longest x1 28.3 us: shards(): lax.all_gather(part_qkv.astype(jnp.bfloat16), ('dp', 'seq'), axis=1, tile...]
    psum x0 -> x1, waiting for transfers between devices: none -> 60.4 us  [shards(): total = lax.psum(own, ('dp', 'seq')).astype(F32)]
  transfers between devices with their start and end apart: 16 -> 6, of which waited for: 13 -> 5; matrix products, arithmetic and copies ran while one was open for 28% -> 1% of each run, Pallas kernels for 0% -> 16%
where the time goes in v1:
time: 1050 us; the launch traced here: 1040 us
  Pallas kernels  581 us (55%)
  waiting for transfers between devices  359 us (34%)
  local copies, waits for them, and re-layouts  70.2 us (7%)
  between operations  14.6 us (1%)
    pallas_call x1, Pallas kernels, cores_join(): pl.pallas_call(cores_join_kernel, out_shape=sds((n, 2, r, k), x.dtype), i...  145 us
    pallas_call x2, Pallas kernels, chips(): pl.pallas_call(functools.partial(chips_kernel, parts), out_shape=tuple((s...  108 us
    reduce_scatter x1, waiting for transfers between devices, shards(): lax.psum_scatter(dw_half.reshape(nz * part, 2 * width), 'fsdp', scatter_d...  88 us
    reduce_scatter x1, waiting for transfers between devices, shards(): own = lax.psum_scatter(grads, 'fsdp', scatter_dimension=0, tiled=True)  78.4 us
    all_gather x1, waiting for transfers between devices, shards(): pieces = lax.all_gather(piece, 'fsdp', axis=0, tiled=False)  77.7 us
    pallas_call x2, Pallas kernels, heads_in(): pl.pallas_call(functools.partial(heads_in_kernel, parts), out_shape=sds((...  76.4 us
    pallas_call x2, Pallas kernels, heads_out(): pl.pallas_call(functools.partial(heads_out_kernel, parts), out_shape=sds(...  74.1 us
    pallas_call x1, Pallas kernels, expert(): pl.pallas_call(expert_kernel, grid=(hidden // chunk,), out_shape=(sds((so...  62.4 us
  transfers between devices with their start and end apart: 6, of which 5 were waited for; matrix products, arithmetic and copies ran while one was open for 1% of the time, Pallas kernels for 16%

profile of v1, /device:TPU:9, one launch (start us, length us, event | category | flops | bytes accessed | tf_op | source)
XLA Modules:
  0.0 1036.5 jit_solution(3832880388632485617)
XLA Ops:
  7.2 4.8 constant_dynamic-slice_fusion
  23.7 77.7 %all-gather.8.cloned.1.call-done = bf16[1536,1,1536]{2,0,1:T(8,128)(2,1)} async-done(((bf16[384,1,1536]{2,0,1:T(8,128)(2,1)}), bf16[1536,1,1536]{2,0,1:T(8,128)(2,1)}) %all-gather.8.cloned.1.call-update) | async-done | bytes 4718608 | tf_op jit(solution)/shard_map/all_gather | solution.py:682
  101.4 144.6 %cores_join.1 = bf16[4,2,384,1536]{3,2,1,0:T(8,128)(2,1)} custom-call(bf16[4,384,1536]{2,1,0:T(8,128)(2,1)} %bitcast.30), custom_call_target="tpu_custom_call" | custom-call | tf_op jit(solution)/shard_map/cores_join/pallas_call | solution.py:200
  252.7 7.3 front.1.src
  260.0 56.2 %heads_in_3.1.q_ref.k_ref.v_ref = bf16[1536,1152]{1,0:T(8,128)(2,1)} custom-call(bf16[768,2304]{1,0:T(8,128)(2,1)} %front.1.src), custom_call_target="tpu_custom_call" | custom-call | tf_op jit(solution)/shard_map/heads_in_3/pallas_call | solution.py:96
  316.2 21.4 %attend.1 = (bf16[1536,384]{1,0:T(8,128)(2,1)}, f32[6,8,1536]{2,1,0:T(8,128)}) custom-call(s32[1,1536]{1,0:T(1,128)} %broadcast_in_dim.26.seg_row, s32[1536,1]{1,0:T(8,128)} %broadcast_in_dim.33.seg_col, bf16[1536,1152]{1,0:T(8,128)(2,1)} %heads_in_3.1.q_ref.k_ref.v_ref, bf16[1536,1152]{1,0:T(8,128)(2,1)} %heads_in_3.1.q_ref.k_ref.v_ref, ...), custom_call_target="tpu_custom_call" | custom-call | tf_op jit(solution)/shard_map/attend/pallas_call | solution.py:313
  337.6 19.0 %heads_out_1.1.att_ref = bf16[768,768]{1,0:T(8,128)(2,1)} custom-call(bf16[1536,384]{1,0:T(8,128)(2,1)} %get-tuple-element.35.refs_0_.o_ref), custom_call_target="tpu_custom_call" | custom-call | tf_op jit(solution)/shard_map/heads_out_1/pallas_call | solution.py:129
  360.6 7.8 middle.1
  368.4 54.5 %chips_3.2 = (bf16[4,384,768]{2,1,0:T(8,128)(2,1)}, bf16[4,384,768]{2,1,0:T(8,128)(2,1)}, f32[4,8,384]{2,1,0:T(8,128)}) custom-call(bf16[4,384,768]{2,1,0:T(8,128)(2,1)} %get-tuple-element.36.refs_0_, bf16[4,384,768]{2,1,0:T(8,128)(2,1)} %take.1.refs_1_, f32[4,8,384]{2,1,0:T(8,128)} %get-tuple-element.37.refs_2_), custom_call_target="tpu_custom_call" | custom-call | tf_op jit(solution)/shard_map/chips_3/pallas_call | solution.py:169
  422.9 62.4 %expert.1 = (bf16[4,384,768]{2,1,0:T(8,128)(2,1)}, bf16[4,384,768]{2,1,0:T(8,128)(2,1)}, f32[4,8,384]{2,1,0:T(8,128)}, bf16[3072,1536]{1,0:T(8,128)(2,1)}) custom-call(bf16[4,384,768]{2,1,0:T(8,128)(2,1)} %get-tuple-element.38.in_ref, bf16[4,384,768]{2,1,0:T(8,128)(2,1)} %get-tuple-element.39.raw_ref, f32[4,8,384]{2,1,0:T(8,128)} %get-tuple-element.40.gate_ref, ...), custom_call_target="tpu_custom_call" | custom-call | tf_op jit(solution)/shard_map/expert/pallas_call | solution.py:541
  485.4 53.4 %chips_3.3 = (bf16[4,384,768]{2,1,0:T(8,128)(2,1)}, bf16[4,384,768]{2,1,0:T(8,128)(2,1)}, f32[4,8,384]{2,1,0:T(8,128)}) custom-call(bf16[4,384,768]{2,1,0:T(8,128)(2,1)} %get-tuple-element.41.refs_0_, bf16[4,384,768]{2,1,0:T(8,128)(2,1)} %get-tuple-element.42.refs_1_, f32[4,8,384]{2,1,0:T(8,128)} %get-tuple-element.43.refs_2_), custom_call_target="tpu_custom_call" | custom-call | tf_op jit(solution)/shard_map/chips_3/pallas_call | solution.py:169
  538.8 14.6 %after.1 = (bf16[768,768]{1,0:T(8,128)(2,1)}, f32[768,768]{1,0:T(8,128)}, bf16[768,768]{1,0:T(8,128)(2,1)}, bf16[768,768]{1,0:T(8,128)(2,1)}, f32[768,128]{1,0:T(8,128)}, /*index=5*/f32[1,768]{1,0:T(1,128)}) custom-call(bf16[4,384,768]{2,1,0:T(8,128)(2,1)} %get-tuple-element.44.res_ref, bf16[4,384,768]{2,1,0:T(8,128)(2,1)} %get-tuple-element.45.gin_ref, ...), custom_call_target="tpu_custom_call" | custom-call | tf_op jit(solution)/shard_map/after/pallas_call | solution.py:602
  555.0 20.2 %heads_in_1.1.do_ref = bf16[1536,384]{1,0:T(8,128)(2,1)} custom-call(bf16[768,768]{1,0:T(8,128)(2,1)} %get-tuple-element.51.src), custom_call_target="tpu_custom_call" | custom-call | tf_op jit(solution)/shard_map/heads_in_1/pallas_call | solution.py:96
  575.2 35.3 %attend_back.1 = (bf16[1536,384]{1,0:T(8,128)(2,1)}, bf16[1536,384]{1,0:T(8,128)(2,1)}, bf16[1536,384]{1,0:T(8,128)(2,1)}) custom-call(s32[1,1536]{1,0:T(1,128)} %broadcast_in_dim.26.seg_row, s32[1536,1]{1,0:T(8,128)} %broadcast_in_dim.33.seg_col, bf16[1536,1152]{1,0:T(8,128)(2,1)} %heads_in_3.1.q_ref.k_ref.v_ref, ...), custom_call_target="tpu_custom_call" | custom-call | tf_op jit(solution)/shard_map/attend_back/pallas_call | solution.py:379
  610.6 55.1 %heads_out_3.1.gp_ref = bf16[768,2304]{1,0:T(8,128)(2,1)} custom-call(bf16[1536,384]{1,0:T(8,128)(2,1)} %get-tuple-element.52.refs_0_, bf16[1536,384]{1,0:T(8,128)(2,1)} %get-tuple-element.53.refs_1_, bf16[1536,384]{1,0:T(8,128)(2,1)} %get-tuple-element.54.refs_2_), custom_call_target="tpu_custom_call" | custom-call | tf_op jit(solution)/shard_map/heads_out_3/pallas_call | solution.py:129
  665.7 11.6 %tail.1 = (bf16[768,768]{1,0:T(8,128)(2,1)}, bf16[768,2304]{1,0:T(8,128)(2,1)}, f32[1,768]{1,0:T(1,128)}) custom-call(bf16[768,768]{1,0:T(8,128)(2,1)} %bitcast.25, f32[1,768]{1,0:T(1,128)} %copy.82.gain_ref, bf16[768,2304]{1,0:T(8,128)(2,1)} %heads_out_3.1.gp_ref, bf16[768,2304]{1,0:T(8,128)(2,1)} %slice.48.w_ref, f32[768,768]{1,0:T(8,128)} %get-tuple-element.55.gh_ref), custom_call_target="tpu_custom_call" | custom-call | tf_op jit(solution)/shard_map/tail/pallas_call | solution.py:637
  678.3 4.9 pad_maximum_fusion
  683.3 13.2 %cores_sum.1 = bf16[4,384,1536]{2,1,0:T(8,128)(2,1)} custom-call(bf16[4,2,384,1536]{3,2,1,0:T(8,128)(2,1)} %bitcast.27), custom_call_target="tpu_custom_call" | custom-call | tf_op jit(solution)/shard_map/cores_sum/pallas_call | solution.py:229
  696.5 78.4 %reduce-scatter.3.cloned.1.call-done = bf16[192,3200]{1,0:T(8,128)(2,1)} async-done(((bf16[768,3200]{1,0:T(8,128)(2,1)}), bf16[192,3200]{1,0:T(8,128)(2,1)}) %reduce-scatter.3.cloned.1.call-update) | async-done | bytes 1228816 | tf_op jit(solution)/shard_map/reduce_scatter | solution.py:717
  775.0 88.0 %reduce-scatter.5.cloned.1.call-done = bf16[384,1536]{1,0:T(8,128)(2,1)} async-done(((bf16[1536,1536]{1,0:T(8,128)(2,1)}), bf16[384,1536]{1,0:T(8,128)(2,1)}) %reduce-scatter.5.cloned.1.call-update) | async-done | bytes 1179664 | tf_op jit(solution)/shard_map/reduce_scatter | solution.py:701
  863.0 60.4 %all-reduce.7.cloned.1.call-done = bf16[192,3200]{1,0:T(8,128)(2,1)} async-done(((bf16[192,3200]{1,0:T(8,128)(2,1)}), bf16[192,3200]{1,0:T(8,128)(2,1)}) %all-reduce.7.cloned.1.call-update) | async-done | bytes 1228816 | tf_op jit(solution)/shard_map/psum | solution.py:718
  929.6 54.9 %all-gather.10.cloned.1.call-done = bf16[3072,1536]{1,0:T(8,128)(2,1)} async-done(((bf16[384,1536]{1,0:T(8,128)(2,1)}), bf16[3072,1536]{1,0:T(8,128)(2,1)}) %all-gather.10.cloned.1.call-update) | async-done | bytes 9437200 | tf_op jit(solution)/shard_map/all_gather | solution.py:710
  984.6 20.1 %copy.101 = f32[2,2,2,384,1536]{4,2,0,3,1:T(2,128)} copy(bf16[2,2,2,384,1536]{4,3,2,1,0:T(8,128)(2,1)} %bitcast.26) | data formatting | bytes 28311552 | tf_op jit(solution)/shard_map/convert_element_type | solution.py:712
  1004.6 24.8 %reshape.33 = f32[768,4,1536]{2,1,0:T(4,128)} reshape(f32[2,384,2,2,1536]{4,3,2,1,0:T(2,128)} %bitcast.20) | data formatting | bytes 37748736 | tf_op jit(solution)/shard_map/convert_element_type | solution.py:712
  (64 shorter events, 31.5 us)
Async XLA Ops:
  7.2 94.2 %all-gather.8.cloned.1.call-start = ((), (), s32[]{:S(2)}) async-start(), calls=%async_computation.6 | async-start | bytes 5898240 | tf_op jit(solution)/shard_map/all_gather | solution.py:682
  12.0 1.3 copy-start.5
  12.0 1.3 copy-start.7
  12.0 1.5 copy-start.2
  12.0 1.7 copy-start.3
  13.2 1.7 copy-start.6
  13.3 3.4 copy-start.4
  13.3 232.7 %all-gather.6.cloned.1.call-start = ((), (), s32[]{:S(2)}) async-start(), calls=%async_computation.2 | async-start | bytes 6144000 | tf_op jit(solution)/shard_map/all_gather | solution.py:674
  14.8 760.1 %reduce-scatter.3.cloned.1.call-start = ((), (), s32[]{:S(2)}) async-start(), calls=%async_computation.3 | async-start | bytes 6144000 | tf_op jit(solution)/shard_map/reduce_scatter | solution.py:717
  665.7 12.6 %copy-start.1 = (bf16[768,768]{1,0:T(8,128)(2,1)S(1)}, bf16[768,768]{1,0:T(8,128)(2,1)}, u32[]{:S(2)}) copy-start(bf16[768,768]{1,0:T(8,128)(2,1)} %get-tuple-element.58) | copy-start | bytes 3538948
  683.2 179.8 %reduce-scatter.5.cloned.1.call-start = ((), (), s32[]{:S(2)}) async-start(), calls=%async_computation.5 | async-start | bytes 5898240 | tf_op jit(solution)/shard_map/reduce_scatter | solution.py:701
  696.5 226.9 %all-reduce.7.cloned.1.call-start = ((), (), s32[]{:S(2)}) async-start(), calls=%async_computation.4 | async-start | bytes 2457600 | tf_op jit(solution)/shard_map/psum | solution.py:718
  775.0 209.6 %all-gather.10.cloned.1.call-start = ((), (), s32[]{:S(2)}) async-start(), calls=%async_computation.7 | async-start | bytes 10616832 | tf_op jit(solution)/shard_map/all_gather | solution.py:710
  923.4 4.9 copy-start
Sparse Core Ops, SparseCore 0:
  13.4 87.9 all-gather.7
  103.5 91.0 all-gather.5
  683.3 91.5 reduce-scatter.2
  777.2 85.7 reduce-scatter.4
  866.4 56.9 all-reduce.6
  925.1 59.4 all-gather.9
